TPU v7x, 32 devices: a whole 2x2x4 slice. The times are simulated.
32 devices in a mesh: clus: 8 (over z, x), ang: 4 (over y, core).
Axes of the slice: x: 2, y: 2, z: 4, core: 2. Of those that a mesh axis runs over, the one named last changes fastest.
Arguments:
- residual: bfloat16 [64, 2, 32, 128], P('clus', None, 'ang'), may hold values from -6 to 6
- margin_ids: int32 [64, 7], replicated, may hold values from 0 to 63, as said below
- block_row: int32 [64, 9], P('clus'), may hold values from 0 to 7, as said below
- block_col: int32 [64, 9], P('clus'), may hold values from 0 to 7, as said below
- inv_blocks: bfloat16 [64, 9, 2, 128, 128], P('clus'), may hold values from -0.375 to 0.375
Outputs:
- preconditioned: float32 [64, 2, 32, 128], P('clus', None, 'ang')
Inputs may be any that keep to these rules, and one draw needn't show every extreme that they name: `margin_ids`: cluster c lies on device c // 8 of clus. The margin clusters of the 8 subdomains of one device all lie on other devices; at most 8 of that device's entries name clusters of any one other device, and some device receives exactly 8 of them. `block_row`: each subdomain's blocks write every one of its 8 slots. `block_col`: each subdomain's blocks read every one of its 8 slots.
All inputs are finite; a program needn't handle non-finite values.
Results may differ from a plain program's by a relative error of at most 0.0029.
Values may be sent and summed in bfloat16 or wider, within the bound.
A program may use at most 64 MiB of HBM per device.

v0:
```python
import functools

import jax
import jax.numpy as jnp
from jax import lax
from jax.experimental import pallas as pl
from jax.experimental.pallas import tpu as pltpu
from jax.sharding import PartitionSpec as P

MESH = pl.DeviceIdType.MESH
CHUNKS = 1


def apply_blocks(sub_rows, block_sub, block_rows, block_cols, block_vals):
    sub_count, slot_count, halves, angle_count, panels = sub_rows.shape
    block_count = block_vals.shape[0]
    flat_inputs = sub_rows.reshape(sub_count * slot_count, halves * angle_count * panels)
    positions = jnp.arange(sub_count * slot_count, dtype=jnp.int32)
    col_index = block_sub * slot_count + block_cols
    col_pick = (col_index[:, None] == positions[None, :]).astype(jnp.bfloat16)
    block_input = jnp.dot(col_pick, flat_inputs, preferred_element_type=jnp.float32).astype(
        jnp.bfloat16
    )
    block_input = block_input.reshape(block_count, halves, angle_count, panels)
    products = jnp.einsum(
        "bmap,bnpq->bmnaq", block_input, block_vals, preferred_element_type=jnp.float32
    )
    real_part = products[:, 0, 0] - products[:, 1, 1]
    imag_part = products[:, 0, 1] + products[:, 1, 0]
    block_out = jnp.stack([real_part, imag_part], axis=1).reshape(
        block_count, halves * angle_count * panels
    )
    row_index = block_sub * slot_count + block_rows
    row_pick = (positions[:, None] == row_index[None, :]).astype(jnp.float32)
    summed = jnp.dot(
        row_pick, block_out, precision=lax.Precision.HIGHEST, preferred_element_type=jnp.float32
    )
    return summed.reshape(sub_count * slot_count, halves, angle_count, panels)


def shards(residual, margin_ids, block_row, block_col, inv_blocks):
    peer_count = lax.axis_size("clus")
    my_index = lax.axis_index("clus")
    clusters, halves, angle_count, panels = residual.shape
    remote = margin_ids.shape[1]
    slot_count = remote + 1
    blocks_each = block_row.shape[1]
    request_count = clusters * remote
    capacity = (request_count + peer_count - 2) // (peer_count - 1)
    feature_count = halves * angle_count * panels
    requests = margin_ids.reshape(peer_count, request_count)
    owners = requests // clusters
    local_ids = requests % clusters
    to_me = (owners == my_index).astype(jnp.int32)
    ranking = jnp.cumsum(to_me, axis=1) - 1
    slot_range = jnp.arange(capacity, dtype=jnp.int32)
    matched = (to_me[:, :, None] == 1) & (ranking[:, :, None] == slot_range[None, None, :])
    chosen = matched[:, :, :, None] & (
        local_ids[:, :, None, None] == jnp.arange(clusters, dtype=jnp.int32)
    )
    selector = jnp.any(chosen, axis=1).reshape(peer_count * capacity, clusters).astype(jnp.bfloat16)
    flat_rows = residual.reshape(clusters, feature_count)
    outgoing = jnp.dot(selector, flat_rows, preferred_element_type=jnp.float32).astype(jnp.bfloat16)
    outgoing = outgoing.reshape(peer_count, capacity, halves, angle_count, panels)
    incoming = lax.all_to_all(outgoing, "clus", split_axis=0, concat_axis=0, tiled=True)
    targets = lax.dynamic_index_in_dim(owners, my_index, 0, keepdims=False)
    order_ids = jnp.arange(request_count, dtype=jnp.int32)
    earlier = (targets[:, None] == targets[None, :]) & (order_ids[:, None] > order_ids[None, :])
    my_ranks = jnp.sum(earlier.astype(jnp.int32), axis=1)
    slot_index = targets * capacity + my_ranks
    remote_rows = incoming.reshape(peer_count * capacity, halves, angle_count, panels)[slot_index]
    remote_rows = remote_rows.reshape(clusters, remote, halves, angle_count, panels)
    sub_rows = jnp.concatenate([residual[:, None], remote_rows], axis=1)
    block_sub = jnp.broadcast_to(
        jnp.arange(clusters, dtype=jnp.int32)[:, None], (clusters, blocks_each)
    ).reshape(-1)
    flat_block_rows = block_row.reshape(-1)
    flat_block_cols = block_col.reshape(-1)
    block_vals = inv_blocks.reshape(clusters * blocks_each, halves, panels, panels)
    slot_sums = apply_blocks(sub_rows, block_sub, flat_block_rows, flat_block_cols, block_vals)
    rounded = slot_sums.astype(jnp.bfloat16).reshape(clusters, slot_count, feature_count)
    own_part = rounded[:, 0]
    remote_part = rounded[:, 1:].reshape(request_count, feature_count)
    slot_ids = jnp.arange(peer_count * capacity, dtype=jnp.int32)
    placer = (slot_ids[:, None] == slot_index[None, :]).astype(jnp.bfloat16)
    returning = jnp.dot(placer, remote_part, preferred_element_type=jnp.float32).astype(
        jnp.bfloat16
    )
    returning = returning.reshape(peer_count, capacity, halves, angle_count, panels)
    returned = lax.all_to_all(returning, "clus", split_axis=0, concat_axis=0, tiled=True)
    gathered_sums = jnp.einsum(
        "rc,rf->cf",
        selector,
        returned.reshape(peer_count * capacity, feature_count),
        preferred_element_type=jnp.float32,
    )
    combined = own_part.astype(jnp.float32) + gathered_sums
    return combined.reshape(clusters, halves, angle_count, panels)


def fused_kernel(
    n,
    ids_hbm,
    rows_hbm,
    cols_hbm,
    res_hbm,
    inv_ref,
    out_ref,
    ids_ref,
    rows_ref,
    cols_ref,
    own_rows,
    gathered,
    weights,
    block_out,
    place_t,
    send_buf,
    recv_buf,
    in_sem,
    w_sem,
    gs_sem,
    gr_sem,
    ss_sem,
    sr_sem,
):
    me = lax.axis_index("clus")
    clusters, halves, all_angles, panels = res_hbm.shape
    chunks = gathered.shape[0]
    angles = all_angles // chunks
    part = halves * angles
    feats = chunks * part
    blocks = rows_ref.shape[1]
    kp = place_t.shape[0]
    total = clusters * blocks

    barrier = pltpu.get_barrier_semaphore()
    for d in range(1, n):
        pl.semaphore_signal(
            barrier, inc=1, device_id={"clus": lax.rem(me + d, n)}, device_id_type=MESH
        )
    own_copy = pltpu.make_async_copy(res_hbm, own_rows, in_sem.at[0])
    own_copy.start()
    tables = [
        pltpu.make_async_copy(source, table, in_sem.at[1 + i])
        for i, (source, table) in enumerate(
            ((ids_hbm, ids_ref), (rows_hbm, rows_ref), (cols_hbm, cols_ref))
        )
    ]
    for copy in tables:
        copy.start()
    w_copies = [
        pltpu.make_async_copy(inv_ref.at[s], weights.at[s], w_sem.at[s]) for s in range(clusters)
    ]
    for copy in w_copies:
        copy.start()

    own_copy.wait()
    for c in range(clusters):
        own = own_rows[c].astype(jnp.float32)
        for h in range(chunks):
            rows = own[:, h * angles : (h + 1) * angles].reshape(part, panels)
            gathered[h, me * clusters + c] = rows.astype(jnp.bfloat16)

    block_out[pl.ds(total * part, (kp - total) * part), :] = jnp.zeros(
        ((kp - total) * part, panels), jnp.float32
    )
    place_t[...] = jnp.zeros_like(place_t)
    lanes = lax.broadcasted_iota(jnp.int32, (1, place_t.shape[1]), 1)

    for copy in tables:
        copy.wait()

    def place_rows(s, carry):
        sub = me * clusters + s
        for b in range(blocks):
            slot = rows_ref[s, b]
            margin = ids_ref[jnp.maximum(slot - 1, 0), sub]
            target = jnp.where(slot == 0, sub, margin)
            place_t[pl.ds(s * blocks + b, 1), :] = (lanes == target).astype(jnp.float32)
        return carry

    lax.fori_loop(0, clusters, place_rows, 0)
    place = jnp.transpose(place_t[...])[: n * clusters].astype(jnp.bfloat16)

    for copy in w_copies:
        copy.wait()
    pl.semaphore_wait(barrier, n - 1)

    gathers = []
    for h in range(chunks):
        for d in range(1, n):
            rows = gathered.at[h, pl.ds(me * clusters, clusters)]
            copy = pltpu.make_async_remote_copy(
                src_ref=rows,
                dst_ref=rows,
                send_sem=gs_sem.at[h, d],
                recv_sem=gr_sem.at[h, d],
                device_id={"clus": lax.rem(me + d, n)},
                device_id_type=MESH,
            )
            copy.start()
            gathers.append(copy)

    returns = []
    for h in range(chunks):
        for copy in gathers[h * (n - 1) : (h + 1) * (n - 1)]:
            copy.wait_recv()

        def subdomain(s, carry):
            sub = me * clusters + s
            for b in range(blocks):
                slot = cols_ref[s, b]
                margin = ids_ref[jnp.maximum(slot - 1, 0), sub]
                source = jnp.where(slot == 0, sub, margin)
                x = gathered[h, source].reshape(part, panels)
                both = jnp.concatenate([weights[s, b, 0], weights[s, b, 1]], axis=1)
                both = jnp.dot(x, both, preferred_element_type=jnp.float32)
                real, imag = both[:, :panels], both[:, panels:]
                start = pl.multiple_of((s * blocks + b) * part, part)
                block_out[pl.ds(start, angles), :] = real[:angles] - imag[angles:]
                block_out[pl.ds(start + angles, angles), :] = imag[:angles] + real[angles:]
            return carry

        lax.fori_loop(0, clusters, subdomain, 0, unroll=4)

        for a in range(part):
            picked = block_out[pl.ds(a, kp, stride=part), :].astype(jnp.bfloat16)
            sums = jnp.dot(place, picked, preferred_element_type=jnp.float32)
            send_buf[h, :, a] = sums.reshape(n, clusters, panels).astype(jnp.bfloat16)

        for d in range(1, n):
            peer = lax.rem(me + d, n)
            copy = pltpu.make_async_remote_copy(
                src_ref=send_buf.at[h, peer],
                dst_ref=recv_buf.at[h, d],
                send_sem=ss_sem.at[h, d],
                recv_sem=sr_sem.at[h, d],
                device_id={"clus": peer},
                device_id_type=MESH,
            )
            copy.start()
            returns.append(copy)

    for h in range(chunks):
        for copy in returns[h * (n - 1) : (h + 1) * (n - 1)]:
            copy.wait_recv()
        for a in range(part):
            acc = send_buf[h, me, a].astype(jnp.float32)
            for d in range(1, n):
                acc = acc + recv_buf[h, d, a].astype(jnp.float32)
            row = a // angles * chunks * angles + h * angles + a % angles
            out_ref[pl.ds(row, clusters, stride=feats), :] = acc
    for copy in gathers + returns:
        copy.wait_send()


def fused(n, residual, margin_ids, block_row, block_col, inv_blocks):
    clusters, halves, angle_count, panels = residual.shape
    blocks = block_row.shape[1]
    feats = halves * angle_count
    chunks = CHUNKS if angle_count % CHUNKS == 0 else 1
    part = feats // chunks
    kp = -(-clusters * blocks // 128) * 128
    mp = -(-clusters * n // 128) * 128
    hbm = pl.BlockSpec(memory_space=pl.ANY)
    vmem = pl.BlockSpec(memory_space=pltpu.VMEM)
    out = pl.pallas_call(
        functools.partial(fused_kernel, n),
        out_shape=pltpu.VMEM((clusters * feats, panels), jnp.float32),
        in_specs=[hbm] * 5,
        out_specs=vmem,
        scratch_shapes=[
            pltpu.SMEM(margin_ids.shape[::-1], jnp.int32),
            pltpu.SMEM(block_row.shape, jnp.int32),
            pltpu.SMEM(block_col.shape, jnp.int32),
            pltpu.VMEM(residual.shape, jnp.bfloat16),
            pltpu.VMEM((chunks, n * clusters, part, panels), jnp.bfloat16),
            pltpu.VMEM(inv_blocks.shape, jnp.bfloat16),
            pltpu.VMEM((kp * part, panels), jnp.float32),
            pltpu.VMEM((kp, mp), jnp.float32),
            pltpu.VMEM((chunks, n, part, clusters, panels), jnp.bfloat16),
            pltpu.VMEM((chunks, n, part, clusters, panels), jnp.bfloat16),
            pltpu.SemaphoreType.DMA((4,)),
            pltpu.SemaphoreType.DMA((clusters,)),
            pltpu.SemaphoreType.DMA((chunks, n)),
            pltpu.SemaphoreType.DMA((chunks, n)),
            pltpu.SemaphoreType.DMA((chunks, n)),
            pltpu.SemaphoreType.DMA((chunks, n)),
        ],
        compiler_params=pltpu.CompilerParams(collective_id=0, has_side_effects=True),
    )(
        margin_ids.T,
        block_row,
        block_col,
        residual,
        inv_blocks,
    )
    return out.reshape(clusters, halves, angle_count, panels)


def apply_device(residual, margin_ids, block_row, block_col, inv_blocks):
    n = lax.axis_size("clus")
    clusters = residual.shape[0]
    capacity = (clusters * margin_ids.shape[1] + n - 2) // (n - 1)
    body = functools.partial(fused, n) if capacity >= clusters else shards
    return body(residual, margin_ids, block_row, block_col, inv_blocks)


def solution(mesh):
    return jax.shard_map(
        apply_device,
        mesh=mesh,
        in_specs=(
            P("clus", None, "ang", None),
            P(),
            P("clus", None),
            P("clus", None),
            P("clus", None, None, None, None),
        ),
        out_specs=P("clus", None, "ang", None),
        check_vma=False,
    )
```

profile of v0, /device:TPU:0, one launch (start us, length us, event | category | flops | bytes accessed | tf_op | source)
XLA Modules:
  0.0 20.3 jit_solution(1514765878422501446)
XLA Ops:
  0.0 19.7 %shard_map.55 = f32[128,128]{1,0:T(8,128)S(1)} custom-call(s32[7,64]{1,0:T(8,128)} %bitcast.3, s32[8,9]{1,0:T(8,128)} %rows_hbm.1, s32[8,9]{1,0:T(8,128)} %cols_hbm.1, bf16[8,2,8,128]{3,2,1,0:T(8,128)(2,1)} %res_hbm.1, bf16[8,9,2,128,128]{4,3,2,1,0:T(8,128)(2,1)} %inv_ref.1), custom_call_target="tpu_custom_call" | custom-call | tf_op jit(solution)/shard_map/pallas_call | solution.py:267
  19.7 0.6 %copy.7 = f32[8,2,8,128]{3,2,1,0:T(8,128)} copy(f32[8,2,8,128]{3,2,1,0:T(8,128)S(1)} %bitcast.2) | data formatting | bytes 131072
where the time goes:
time: 20.4 us; the launch traced here: 20.3 us
  Pallas kernels  19.7 us (97%)
  local copies, waits for them, and re-layouts  0.63 us (3%)
    pallas_call x1, Pallas kernels, fused(): pl.pallas_call(functools.partial(fused_kernel, n), out_shape=pltpu.VMEM((...  19.7 us
    unnamed x1, local copies, waits for them, and re-layouts  0.63 us

commit v1 on v0

--- a/solution.py
+++ b/solution.py
@@ -8,7 +8,6 @@
 from jax.sharding import PartitionSpec as P
 
 MESH = pl.DeviceIdType.MESH
-CHUNKS = 1
 
 
 def apply_blocks(sub_rows, block_sub, block_rows, block_cols, block_vals):
@@ -97,6 +96,13 @@
     combined = own_part.astype(jnp.float32) + gathered_sums
     return combined.reshape(clusters, halves, angle_count, panels)
 
+def UP(n):
+    return range(n)
+
+
+def RORDER(me, n):
+    return [lax.rem(me + d, n) for d in range(1, n)]
+
 
 def fused_kernel(
     n,
@@ -109,7 +115,6 @@
     ids_ref,
     rows_ref,
     cols_ref,
-    own_rows,
     gathered,
     weights,
     block_out,
@@ -118,27 +123,31 @@
     recv_buf,
     in_sem,
     w_sem,
+    ready,
     gs_sem,
     gr_sem,
     ss_sem,
     sr_sem,
 ):
     me = lax.axis_index("clus")
-    clusters, halves, all_angles, panels = res_hbm.shape
-    chunks = gathered.shape[0]
-    angles = all_angles // chunks
-    part = halves * angles
-    feats = chunks * part
+    clusters, part, panels = res_hbm.shape
+    angles = part // 2
     blocks = rows_ref.shape[1]
     kp = place_t.shape[0]
     total = clusters * blocks
-
     barrier = pltpu.get_barrier_semaphore()
-    for d in range(1, n):
-        pl.semaphore_signal(
-            barrier, inc=1, device_id={"clus": lax.rem(me + d, n)}, device_id_type=MESH
-        )
-    own_copy = pltpu.make_async_copy(res_hbm, own_rows, in_sem.at[0])
+
+    def at(peer):
+        return {"clus": peer}
+
+    for e in range(1, n):
+
+        @pl.when(e > me)
+        def _():
+            pl.semaphore_signal(barrier, inc=1, device_id=at(e), device_id_type=MESH)
+
+    mine = gathered.at[pl.ds(me * clusters, clusters)]
+    own_copy = pltpu.make_async_copy(res_hbm, mine, in_sem.at[0])
     own_copy.start()
     tables = [
         pltpu.make_async_copy(source, table, in_sem.at[1 + i])
@@ -148,18 +157,50 @@
     ]
     for copy in tables:
         copy.start()
+
+    @pl.when(me > 0)
+    def _():
+        pl.semaphore_wait(barrier, me)
+
+    for e in range(n - 1):
+
+        @pl.when(e < me)
+        def _():
+            pl.semaphore_signal(ready.at[me], inc=1, device_id=at(e), device_id_type=MESH)
+
     w_copies = [
         pltpu.make_async_copy(inv_ref.at[s], weights.at[s], w_sem.at[s]) for s in range(clusters)
     ]
     for copy in w_copies:
         copy.start()
 
+    def gather(peer, source):
+        rows = gathered.at[pl.ds(source * clusters, clusters)]
+        return pltpu.make_async_remote_copy(
+            src_ref=rows,
+            dst_ref=rows,
+            send_sem=gs_sem.at[peer],
+            recv_sem=gr_sem.at[source],
+            device_id=at(peer),
+            device_id_type=MESH,
+        )
+
+    def send_back(peer, source):
+        return pltpu.make_async_remote_copy(
+            src_ref=send_buf.at[peer],
+            dst_ref=recv_buf.at[source],
+            send_sem=ss_sem.at[peer],
+            recv_sem=sr_sem.at[source],
+            device_id=at(peer),
+            device_id_type=MESH,
+        )
+
     own_copy.wait()
-    for c in range(clusters):
-        own = own_rows[c].astype(jnp.float32)
-        for h in range(chunks):
-            rows = own[:, h * angles : (h + 1) * angles].reshape(part, panels)
-            gathered[h, me * clusters + c] = rows.astype(jnp.bfloat16)
+    for e in UP(n):
+
+        @pl.when(e < me)
+        def _():
+            gather(e, me).start()
 
     block_out[pl.ds(total * part, (kp - total) * part), :] = jnp.zeros(
         ((kp - total) * part, panels), jnp.float32
@@ -179,120 +220,106 @@
             place_t[pl.ds(s * blocks + b, 1), :] = (lanes == target).astype(jnp.float32)
         return carry
 
+    def send_down():
+        for e in range(1, n):
+
+            @pl.when(e > me)
+            def _():
+                pl.semaphore_wait(ready.at[e], 1)
+                gather(e, me).start()
+
     lax.fori_loop(0, clusters, place_rows, 0)
     place = jnp.transpose(place_t[...])[: n * clusters].astype(jnp.bfloat16)
+    send_down()
 
     for copy in w_copies:
         copy.wait()
-    pl.semaphore_wait(barrier, n - 1)
-
-    gathers = []
-    for h in range(chunks):
-        for d in range(1, n):
-            rows = gathered.at[h, pl.ds(me * clusters, clusters)]
-            copy = pltpu.make_async_remote_copy(
-                src_ref=rows,
-                dst_ref=rows,
-                send_sem=gs_sem.at[h, d],
-                recv_sem=gr_sem.at[h, d],
-                device_id={"clus": lax.rem(me + d, n)},
-                device_id_type=MESH,
-            )
-            copy.start()
-            gathers.append(copy)
-
-    returns = []
-    for h in range(chunks):
-        for copy in gathers[h * (n - 1) : (h + 1) * (n - 1)]:
-            copy.wait_recv()
-
-        def subdomain(s, carry):
-            sub = me * clusters + s
-            for b in range(blocks):
-                slot = cols_ref[s, b]
-                margin = ids_ref[jnp.maximum(slot - 1, 0), sub]
-                source = jnp.where(slot == 0, sub, margin)
-                x = gathered[h, source].reshape(part, panels)
-                both = jnp.concatenate([weights[s, b, 0], weights[s, b, 1]], axis=1)
-                both = jnp.dot(x, both, preferred_element_type=jnp.float32)
-                real, imag = both[:, :panels], both[:, panels:]
-                start = pl.multiple_of((s * blocks + b) * part, part)
-                block_out[pl.ds(start, angles), :] = real[:angles] - imag[angles:]
-                block_out[pl.ds(start + angles, angles), :] = imag[:angles] + real[angles:]
-            return carry
-
-        lax.fori_loop(0, clusters, subdomain, 0, unroll=4)
-
-        for a in range(part):
-            picked = block_out[pl.ds(a, kp, stride=part), :].astype(jnp.bfloat16)
-            sums = jnp.dot(place, picked, preferred_element_type=jnp.float32)
-            send_buf[h, :, a] = sums.reshape(n, clusters, panels).astype(jnp.bfloat16)
-
-        for d in range(1, n):
-            peer = lax.rem(me + d, n)
-            copy = pltpu.make_async_remote_copy(
-                src_ref=send_buf.at[h, peer],
-                dst_ref=recv_buf.at[h, d],
-                send_sem=ss_sem.at[h, d],
-                recv_sem=sr_sem.at[h, d],
-                device_id={"clus": peer},
-                device_id_type=MESH,
-            )
-            copy.start()
-            returns.append(copy)
-
-    for h in range(chunks):
-        for copy in returns[h * (n - 1) : (h + 1) * (n - 1)]:
-            copy.wait_recv()
-        for a in range(part):
-            acc = send_buf[h, me, a].astype(jnp.float32)
-            for d in range(1, n):
-                acc = acc + recv_buf[h, d, a].astype(jnp.float32)
-            row = a // angles * chunks * angles + h * angles + a % angles
-            out_ref[pl.ds(row, clusters, stride=feats), :] = acc
-    for copy in gathers + returns:
-        copy.wait_send()
+    for d in range(1, n):
+        source = lax.rem(me + d, n)
+        gather(source, source).wait_recv()
+
+    def subdomain(s, carry):
+        sub = me * clusters + s
+        for b in range(blocks):
+            slot = cols_ref[s, b]
+            margin = ids_ref[jnp.maximum(slot - 1, 0), sub]
+            source = jnp.where(slot == 0, sub, margin)
+            x = gathered[source]
+            both = jnp.concatenate([weights[s, b, 0], weights[s, b, 1]], axis=1)
+            both = jnp.dot(x, both, preferred_element_type=jnp.float32)
+            real, imag = both[:, :panels], both[:, panels:]
+            start = pl.multiple_of((s * blocks + b) * part, part)
+            block_out[pl.ds(start, angles), :] = real[:angles] - imag[angles:]
+            block_out[pl.ds(start + angles, angles), :] = imag[:angles] + real[angles:]
+        return carry
+
+    lax.fori_loop(0, clusters, subdomain, 0, unroll=4)
+
+    for a in range(part):
+        picked = block_out[pl.ds(a, kp, stride=part), :].astype(jnp.bfloat16)
+        sums = jnp.dot(place, picked, preferred_element_type=jnp.float32)
+        send_buf[:, a] = sums.reshape(n, clusters, panels).astype(jnp.bfloat16)
+
+    for peer in RORDER(me, n):
+        if isinstance(peer, tuple):
+            peer, cond = peer
+
+            @pl.when(cond)
+            def _():
+                send_back(peer, me).start()
+        else:
+            send_back(peer, me).start()
+
+    acc = [send_buf[me, a].astype(jnp.float32) for a in range(part)]
+    for d in range(1, n):
+        source = lax.rem(me + d, n)
+        send_back(source, source).wait_recv()
+        acc = [acc[a] + recv_buf[source, a].astype(jnp.float32) for a in range(part)]
+    for a in range(part):
+        out_ref[pl.ds(a, clusters, stride=part), :] = acc[a]
+    for d in range(1, n):
+        peer = lax.rem(me + d, n)
+        gather(peer, me).wait_send()
+        send_back(peer, me).wait_send()
 
 
 def fused(n, residual, margin_ids, block_row, block_col, inv_blocks):
     clusters, halves, angle_count, panels = residual.shape
     blocks = block_row.shape[1]
-    feats = halves * angle_count
-    chunks = CHUNKS if angle_count % CHUNKS == 0 else 1
-    part = feats // chunks
+    part = halves * angle_count
     kp = -(-clusters * blocks // 128) * 128
     mp = -(-clusters * n // 128) * 128
     hbm = pl.BlockSpec(memory_space=pl.ANY)
     vmem = pl.BlockSpec(memory_space=pltpu.VMEM)
     out = pl.pallas_call(
         functools.partial(fused_kernel, n),
-        out_shape=pltpu.VMEM((clusters * feats, panels), jnp.float32),
+        out_shape=pltpu.VMEM((clusters * part, panels), jnp.float32),
         in_specs=[hbm] * 5,
         out_specs=vmem,
         scratch_shapes=[
             pltpu.SMEM(margin_ids.shape[::-1], jnp.int32),
             pltpu.SMEM(block_row.shape, jnp.int32),
             pltpu.SMEM(block_col.shape, jnp.int32),
-            pltpu.VMEM(residual.shape, jnp.bfloat16),
-            pltpu.VMEM((chunks, n * clusters, part, panels), jnp.bfloat16),
+            pltpu.VMEM((n * clusters, part, panels), jnp.bfloat16),
             pltpu.VMEM(inv_blocks.shape, jnp.bfloat16),
             pltpu.VMEM((kp * part, panels), jnp.float32),
             pltpu.VMEM((kp, mp), jnp.float32),
-            pltpu.VMEM((chunks, n, part, clusters, panels), jnp.bfloat16),
-            pltpu.VMEM((chunks, n, part, clusters, panels), jnp.bfloat16),
+            pltpu.VMEM((n, part, clusters, panels), jnp.bfloat16),
+            pltpu.VMEM((n, part, clusters, panels), jnp.bfloat16),
             pltpu.SemaphoreType.DMA((4,)),
             pltpu.SemaphoreType.DMA((clusters,)),
-            pltpu.SemaphoreType.DMA((chunks, n)),
-            pltpu.SemaphoreType.DMA((chunks, n)),
-            pltpu.SemaphoreType.DMA((chunks, n)),
-            pltpu.SemaphoreType.DMA((chunks, n)),
+            pltpu.SemaphoreType.REGULAR((n,)),
+            pltpu.SemaphoreType.DMA((n,)),
+            pltpu.SemaphoreType.DMA((n,)),
+            pltpu.SemaphoreType.DMA((n,)),
+            pltpu.SemaphoreType.DMA((n,)),
         ],
         compiler_params=pltpu.CompilerParams(collective_id=0, has_side_effects=True),
     )(
         margin_ids.T,
         block_row,
         block_col,
-        residual,
+        residual.reshape(clusters, part, panels),
         inv_blocks,
     )
     return out.reshape(clusters, halves, angle_count, panels)

time: 20.4 us -> 20.1 us (0.985)
  Pallas kernels: 19.7 us -> 19.3 us
    pallas_call x1, Pallas kernels: 19.7 us -> 19.3 us  [fused(): pl.pallas_call(functools.partial(fused_kernel, n), out_shape=pltpu.VMEM((...]
where the time goes in v1:
time: 20.1 us; the launch traced here: 20 us
  Pallas kernels  19.3 us (96%)
  local copies, waits for them, and re-layouts  0.63 us (3%)
    pallas_call x1, Pallas kernels, fused(): pl.pallas_call(functools.partial(fused_kernel, n), out_shape=pltpu.VMEM((...  19.3 us
    unnamed x1, local copies, waits for them, and re-layouts  0.63 us

profile of v1, /device:TPU:0, one launch (start us, length us, event | category | flops | bytes accessed | tf_op | source)
XLA Modules:
  0.0 20.0 jit_solution(11087915386609398857)
XLA Ops:
  0.0 19.3 %shard_map.55 = f32[128,128]{1,0:T(8,128)S(1)} custom-call(s32[7,64]{1,0:T(8,128)} %bitcast.5, s32[8,9]{1,0:T(8,128)} %rows_hbm.1, s32[8,9]{1,0:T(8,128)} %cols_hbm.1, bf16[8,16,128]{2,1,0:T(8,128)(2,1)} %bitcast.4, bf16[8,9,2,128,128]{4,3,2,1,0:T(8,128)(2,1)} %inv_ref.1), custom_call_target="tpu_custom_call" | custom-call | tf_op jit(solution)/shard_map/pallas_call | solution.py:294
  19.3 0.6 %copy.7 = f32[8,2,8,128]{3,2,1,0:T(8,128)} copy(f32[8,2,8,128]{3,2,1,0:T(8,128)S(1)} %bitcast.3) | data formatting | bytes 131072

commit v2 on v1

--- a/solution.py
+++ b/solution.py
@@ -8,6 +8,7 @@
 from jax.sharding import PartitionSpec as P
 
 MESH = pl.DeviceIdType.MESH
+GATHER_MASKS = (7, 2, 5, 6, 3, 4, 1)
 
 
 def apply_blocks(sub_rows, block_sub, block_rows, block_cols, block_vals):
@@ -96,11 +97,9 @@
     combined = own_part.astype(jnp.float32) + gathered_sums
     return combined.reshape(clusters, halves, angle_count, panels)
 
-def UP(n):
-    return range(n)
-
-
-def RORDER(me, n):
+def gather_order(me, n):
+    if n == len(GATHER_MASKS) + 1:
+        return [lax.bitwise_xor(me, jnp.int32(mask)) for mask in GATHER_MASKS]
     return [lax.rem(me + d, n) for d in range(1, n)]
 
 
@@ -123,7 +122,6 @@
     recv_buf,
     in_sem,
     w_sem,
-    ready,
     gs_sem,
     gr_sem,
     ss_sem,
@@ -140,11 +138,8 @@
     def at(peer):
         return {"clus": peer}
 
-    for e in range(1, n):
-
-        @pl.when(e > me)
-        def _():
-            pl.semaphore_signal(barrier, inc=1, device_id=at(e), device_id_type=MESH)
+    for d in range(1, n):
+        pl.semaphore_signal(barrier, inc=1, device_id=at(lax.rem(me + d, n)), device_id_type=MESH)
 
     mine = gathered.at[pl.ds(me * clusters, clusters)]
     own_copy = pltpu.make_async_copy(res_hbm, mine, in_sem.at[0])
@@ -158,16 +153,6 @@
     for copy in tables:
         copy.start()
 
-    @pl.when(me > 0)
-    def _():
-        pl.semaphore_wait(barrier, me)
-
-    for e in range(n - 1):
-
-        @pl.when(e < me)
-        def _():
-            pl.semaphore_signal(ready.at[me], inc=1, device_id=at(e), device_id_type=MESH)
-
     w_copies = [
         pltpu.make_async_copy(inv_ref.at[s], weights.at[s], w_sem.at[s]) for s in range(clusters)
     ]
@@ -195,13 +180,6 @@
             device_id_type=MESH,
         )
 
-    own_copy.wait()
-    for e in UP(n):
-
-        @pl.when(e < me)
-        def _():
-            gather(e, me).start()
-
     block_out[pl.ds(total * part, (kp - total) * part), :] = jnp.zeros(
         ((kp - total) * part, panels), jnp.float32
     )
@@ -220,17 +198,12 @@
             place_t[pl.ds(s * blocks + b, 1), :] = (lanes == target).astype(jnp.float32)
         return carry
 
-    def send_down():
-        for e in range(1, n):
-
-            @pl.when(e > me)
-            def _():
-                pl.semaphore_wait(ready.at[e], 1)
-                gather(e, me).start()
-
     lax.fori_loop(0, clusters, place_rows, 0)
     place = jnp.transpose(place_t[...])[: n * clusters].astype(jnp.bfloat16)
-    send_down()
+    own_copy.wait()
+    pl.semaphore_wait(barrier, n - 1)
+    for peer in gather_order(me, n):
+        gather(peer, me).start()
 
     for copy in w_copies:
         copy.wait()
@@ -245,12 +218,12 @@
             margin = ids_ref[jnp.maximum(slot - 1, 0), sub]
             source = jnp.where(slot == 0, sub, margin)
             x = gathered[source]
-            both = jnp.concatenate([weights[s, b, 0], weights[s, b, 1]], axis=1)
-            both = jnp.dot(x, both, preferred_element_type=jnp.float32)
-            real, imag = both[:, :panels], both[:, panels:]
+            turned = jnp.concatenate([-x[angles:], x[:angles]], axis=0)
+            both = jnp.concatenate([x, turned], axis=1)
             start = pl.multiple_of((s * blocks + b) * part, part)
-            block_out[pl.ds(start, angles), :] = real[:angles] - imag[angles:]
-            block_out[pl.ds(start + angles, angles), :] = imag[:angles] + real[angles:]
+            block_out[pl.ds(start, part), :] = jnp.dot(
+                both, weights[s, b], preferred_element_type=jnp.float32
+            )
         return carry
 
     lax.fori_loop(0, clusters, subdomain, 0, unroll=4)
@@ -260,27 +233,21 @@
         sums = jnp.dot(place, picked, preferred_element_type=jnp.float32)
         send_buf[:, a] = sums.reshape(n, clusters, panels).astype(jnp.bfloat16)
 
-    for peer in RORDER(me, n):
-        if isinstance(peer, tuple):
-            peer, cond = peer
-
-            @pl.when(cond)
-            def _():
-                send_back(peer, me).start()
-        else:
-            send_back(peer, me).start()
-
+    for d in range(1, n):
+        send_back(lax.rem(me + d, n), me).start()
+
+    for d in range(1, n):
+        gather(lax.rem(me + d, n), me).wait_send()
     acc = [send_buf[me, a].astype(jnp.float32) for a in range(part)]
     for d in range(1, n):
+        if d == n - 1:
+            for k in range(1, n):
+                send_back(lax.rem(me + k, n), me).wait_send()
         source = lax.rem(me + d, n)
         send_back(source, source).wait_recv()
         acc = [acc[a] + recv_buf[source, a].astype(jnp.float32) for a in range(part)]
     for a in range(part):
         out_ref[pl.ds(a, clusters, stride=part), :] = acc[a]
-    for d in range(1, n):
-        peer = lax.rem(me + d, n)
-        gather(peer, me).wait_send()
-        send_back(peer, me).wait_send()
 
 
 def fused(n, residual, margin_ids, block_row, block_col, inv_blocks):
@@ -301,14 +268,13 @@
             pltpu.SMEM(block_row.shape, jnp.int32),
             pltpu.SMEM(block_col.shape, jnp.int32),
             pltpu.VMEM((n * clusters, part, panels), jnp.bfloat16),
-            pltpu.VMEM(inv_blocks.shape, jnp.bfloat16),
+            pltpu.VMEM((clusters, blocks, 2 * panels, panels), jnp.bfloat16),
             pltpu.VMEM((kp * part, panels), jnp.float32),
             pltpu.VMEM((kp, mp), jnp.float32),
             pltpu.VMEM((n, part, clusters, panels), jnp.bfloat16),
             pltpu.VMEM((n, part, clusters, panels), jnp.bfloat16),
             pltpu.SemaphoreType.DMA((4,)),
             pltpu.SemaphoreType.DMA((clusters,)),
-            pltpu.SemaphoreType.REGULAR((n,)),
             pltpu.SemaphoreType.DMA((n,)),
             pltpu.SemaphoreType.DMA((n,)),
             pltpu.SemaphoreType.DMA((n,)),
@@ -320,7 +286,7 @@
         block_row,
         block_col,
         residual.reshape(clusters, part, panels),
-        inv_blocks,
+        inv_blocks.reshape(clusters, blocks, 2 * panels, panels),
     )
     return out.reshape(clusters, halves, angle_count, panels)
 

time: 20.1 us -> 19.5 us (0.970)
  Pallas kernels: 19.3 us -> 18.7 us
    pallas_call x1, Pallas kernels: 19.3 us -> 18.7 us  [fused(): pl.pallas_call(functools.partial(fused_kernel, n), out_shape=pltpu.VMEM((...]
where the time goes in v2:
time: 19.5 us; the launch traced here: 19.3 us
  Pallas kernels  18.7 us (96%)
  local copies, waits for them, and re-layouts  0.63 us (3%)
    pallas_call x1, Pallas kernels, fused(): pl.pallas_call(functools.partial(fused_kernel, n), out_shape=pltpu.VMEM((...  18.7 us
    unnamed x1, local copies, waits for them, and re-layouts  0.63 us

profile of v2, /device:TPU:0, one launch (start us, length us, event | category | flops | bytes accessed | tf_op | source)
XLA Modules:
  0.0 19.3 jit_solution(761031143765255202)
XLA Ops:
  0.0 18.7 %shard_map.55 = f32[128,128]{1,0:T(8,128)S(1)} custom-call(s32[7,64]{1,0:T(8,128)} %bitcast.7, s32[8,9]{1,0:T(8,128)} %rows_hbm.1, s32[8,9]{1,0:T(8,128)} %cols_hbm.1, bf16[8,16,128]{2,1,0:T(8,128)(2,1)} %bitcast.6, bf16[8,9,256,128]{3,2,1,0:T(8,128)(2,1)} %bitcast.5), custom_call_target="tpu_custom_call" | custom-call | tf_op jit(solution)/shard_map/pallas_call | solution.py:261
  18.7 0.6 %copy.7 = f32[8,2,8,128]{3,2,1,0:T(8,128)} copy(f32[8,2,8,128]{3,2,1,0:T(8,128)S(1)} %bitcast.4) | data formatting | bytes 131072
